TPU v7x, 32 devices: a whole 2x2x4 slice. The times are simulated.
32 devices in a mesh: groups: 2 (over y), ctx: 4 (over x, core), head: 4 (over z).
Axes of the slice: x: 2, y: 2, z: 4, core: 2. Of those that a mesh axis runs over, the one named last changes fastest.
Arguments:
- tokens_in: bfloat16 [8192, 4096], P(('groups', 'ctx')), parts along dimension 0, may hold values from -16 to 16
- tempo_ids: int32 [8192], P(('groups', 'ctx')), parts along dimension 0, may hold values from 0 to 63
- tempo_table: bfloat16 [64, 4096], replicated, may hold values from -6 to 6
- w_query: bfloat16 [4096, 2048], P('ctx', 'head'), may hold values from -0.1875 to 0.1875
- w_key: bfloat16 [4096, 2048], P('ctx', 'head'), may hold values from -0.09375 to 0.09375
- w_value: bfloat16 [4096, 2048], P('ctx', 'head'), may hold values from -0.09375 to 0.09375
Outputs:
- attended: bfloat16 [8192, 2048], P(('groups', 'ctx'), 'head'), parts along dimension 0
There are 2 independent parts, one for each index of `groups`. A program takes and returns all parts, laid end to end along the dimension named above; an argument that names none is the same for every part. Nothing has to cross between parts.
All inputs are finite; a program needn't handle non-finite values.
Results may differ from a plain program's by a relative error of at most 0.029.
Values may be sent and summed in bfloat16 or wider, within the bound.
No kernel may reach another device: no remote copies, remote signals or barrier semaphores. Data moves between devices by JAX's collectives and lax.ppermute only.
A program may use at most 64 MiB of HBM per device.

v0:
```python
import jax
import jax.numpy as jnp
from jax import lax
from jax.sharding import PartitionSpec as P

HEAD_DIM = 128
SPAN = 1024
BEACONS = 32
POOL = 32
LOWEST = -1e30


def by_heads(matrix, heads_local):
    return matrix.reshape(matrix.shape[0], heads_local, -1).transpose(1, 0, 2)


def partial_attend(queries, keys, values, allowed):
    scores = jnp.einsum(
        "hqd,hkd->hqk", queries, keys, preferred_element_type=jnp.float32
    ) * queries.shape[-1] ** (-0.5)
    masked = jnp.where(allowed, scores, LOWEST)
    highest = jnp.max(masked, axis=2)
    weights = jnp.where(allowed, jnp.exp(masked - highest[..., None]), 0.0)
    totals = jnp.sum(weights, axis=2)
    summed = jnp.einsum(
        "hqk,hkd->hqd", weights.astype(jnp.bfloat16), values, preferred_element_type=jnp.float32
    )
    return (highest, totals, summed)


def combine_partials(first, second):
    highest = jnp.maximum(first[0], second[0])
    left_factor = jnp.exp(first[0] - highest)
    right_factor = jnp.exp(second[0] - highest)
    totals = first[1] * left_factor + second[1] * right_factor
    summed = first[2] * left_factor[..., None] + second[2] * right_factor[..., None]
    return (highest, totals, summed)


def beacon_partial(
    queries, query_span, beacon_keys, beacon_values, low_rank, high_rank, group, slots_dev
):
    heads_local, query_count, head_size = queries.shape
    block_width = group * slots_dev
    start_state = (
        jnp.full((heads_local, query_count), LOWEST, jnp.float32),
        jnp.zeros((heads_local, query_count), jnp.float32),
        jnp.zeros((heads_local, query_count, head_size), jnp.float32),
    )

    def visit(block, state):
        first_slot = block * block_width
        block_keys = lax.dynamic_slice_in_dim(beacon_keys, first_slot, block_width, 1)
        block_values = lax.dynamic_slice_in_dim(beacon_values, first_slot, block_width, 1)
        slot_index = first_slot + jnp.arange(block_width, dtype=jnp.int32)
        owner = slot_index // slots_dev
        in_range = (owner >= low_rank) & (owner < high_rank)
        earlier = (slot_index // BEACONS)[None, :] < query_span[:, None]
        allowed = (in_range[None, :] & earlier)[None]
        return combine_partials(state, partial_attend(queries, block_keys, block_values, allowed))

    first_block = low_rank // group
    last_block = (high_rank + group - 1) // group
    return lax.fori_loop(first_block, last_block, visit, start_state)


def on_device(tokens_in, tempo_ids, tempo_table, w_query, w_key, w_value):
    row_count = tokens_in.shape[0]
    col_width = w_query.shape[1]
    heads_local = col_width // HEAD_DIM
    ctx_count = lax.axis_size("ctx")
    ctx_rank = lax.axis_index("ctx")
    spans_dev = row_count // SPAN
    slots_dev = spans_dev * BEACONS
    target = max(1, 256 // slots_dev)
    group = min(ctx_count, 1 << target.bit_length() - 1)
    selector = (
        tempo_ids[:, None] == jnp.arange(tempo_table.shape[0], dtype=jnp.int32)[None, :]
    ).astype(jnp.bfloat16)
    hidden = (
        tokens_in.astype(jnp.float32)
        + jnp.dot(selector, tempo_table, preferred_element_type=jnp.float32)
    ).astype(jnp.bfloat16)
    pieces = (
        lax.all_gather(w_query, "ctx", axis=0, tiled=True),
        lax.all_gather(w_key, "ctx", axis=0, tiled=True),
        lax.all_gather(w_value, "ctx", axis=0, tiled=True),
    )
    projected = tuple(
        (jnp.dot(hidden, piece, preferred_element_type=jnp.float32) for piece in pieces)
    )
    queries = projected[0].astype(jnp.bfloat16)
    keys = projected[1].astype(jnp.bfloat16)
    values = projected[2].astype(jnp.bfloat16)
    pool_scale = POOL ** (-0.5)
    own_keys = (
        jnp.sum(keys.reshape(slots_dev, POOL, col_width).astype(jnp.float32), axis=1) * pool_scale
    ).astype(jnp.bfloat16)
    own_values = (
        jnp.sum(values.reshape(slots_dev, POOL, col_width).astype(jnp.float32), axis=1) * pool_scale
    ).astype(jnp.bfloat16)
    every_keys, every_values = (
        lax.all_gather(own_keys, "ctx", axis=0, tiled=True),
        lax.all_gather(own_values, "ctx", axis=0, tiled=True),
    )
    beacon_keys = by_heads(every_keys, heads_local)
    beacon_values = by_heads(every_values, heads_local)
    query_heads = by_heads(queries, heads_local)
    local_span = jnp.arange(row_count, dtype=jnp.int32) // SPAN
    own_span = ctx_rank * spans_dev + local_span

    def fold_spans(matrix):
        return by_heads(matrix, heads_local)

    causal = (
        jnp.arange(SPAN, dtype=jnp.int32)[:, None] >= jnp.arange(SPAN, dtype=jnp.int32)[None, :]
    )[None]
    inside = partial_attend(fold_spans(queries), fold_spans(keys), fold_spans(values), causal)
    inside = (inside[0], inside[1], inside[2])
    upper_rank = ctx_rank + 1
    remote = beacon_partial(
        query_heads,
        own_span,
        beacon_keys,
        beacon_values,
        jnp.zeros((), jnp.int32),
        upper_rank,
        group,
        slots_dev,
    )
    highest, totals, summed = combine_partials(inside, remote)
    attended = summed / totals[..., None]
    return attended.transpose(1, 0, 2).reshape(row_count, col_width).astype(jnp.bfloat16)


def solution(mesh):
    in_specs = (
        P(("groups", "ctx"), None),
        P(("groups", "ctx")),
        P(),
        P("ctx", "head"),
        P("ctx", "head"),
        P("ctx", "head"),
    )
    out_specs = P(("groups", "ctx"), "head")
    return jax.shard_map(
        on_device, mesh=mesh, in_specs=in_specs, out_specs=out_specs, check_vma=False
    )
```

profile of v0, /device:TPU:0, one launch (start us, length us, event | category | flops | bytes accessed | tf_op | source)
XLA Modules:
  0.0 165.5 jit_solution(11830383064842661481)
XLA Ops:
  6.5 0.7 all-gather.4.cloned.1.call-update
  7.3 0.7 all-gather.6.cloned.1.call-update
  8.1 0.7 all-gather.8.cloned.1.call-update
  8.8 1.3 iota_compare_fusion
  10.0 6.9 %add_convert_fusion = bf16[1024,4096]{1,0:T(8,128)(2,1)} fusion(bf16[1024,4096]{1,0:T(8,128)(2,1)} %param.8, bf16[64,4096]{1,0:T(8,128)(2,1)S(1)} %copy-done, s32[1024]{0:T(1024)S(1)} %copy-done.3), kind=kOutput, calls=%fused_computation.34 | convolution fusion | flops 549519360 | bytes 17305600 | tf_op jit(solution)/shard_map/dot_general | solution.py:82
  16.9 29.2 %all-gather.4.cloned.1.call-done = bf16[4096,512]{1,0:T(8,128)(2,1)} async-done(((bf16[1024,512]{1,0:T(8,128)(2,1)}), bf16[4096,512]{1,0:T(8,128)(2,1)}) %all-gather.4.cloned.1.call-update) | async-done | bytes 4194320 | tf_op jit(solution)/shard_map/all_gather | solution.py:85
  46.1 9.1 %convolution_convert_fusion.2 = bf16[1024,512]{0,1:T(8,128)(2,1)S(1)} fusion(bf16[1024,4096]{1,0:T(8,128)(2,1)} %add_convert_fusion, bf16[4096,512]{1,0:T(8,128)(2,1)} %all-gather.4.cloned.1.call-done), kind=kOutput, calls=%fused_computation.46 | convolution fusion | flops 4295491584 | bytes 13631488 | tf_op jit(solution)/shard_map/dot_general | solution.py:90
  55.2 1.3 copy.24
  56.5 25.6 %all-gather.6.cloned.1.call-done = bf16[4096,512]{1,0:T(8,128)(2,1)} async-done(((bf16[1024,512]{1,0:T(8,128)(2,1)}), bf16[4096,512]{1,0:T(8,128)(2,1)}) %all-gather.6.cloned.1.call-update) | async-done | bytes 4194320 | tf_op jit(solution)/shard_map/all_gather | solution.py:86
  82.2 10.0 %convert_reduce_fusion.1 = (f32[32,512]{1,0:T(8,128)S(1)}, bf16[1024,512]{1,0:T(8,128)(2,1)}) fusion(bf16[1024,4096]{1,0:T(8,128)(2,1)} %add_convert_fusion, bf16[4096,512]{1,0:T(8,128)(2,1)} %all-gather.6.cloned.1.call-done), kind=kOutput, calls=%fused_computation.42 | convolution fusion | flops 4296523776 | bytes 13697024 | tf_op jit(solution)/shard_map/dot_general | solution.py:90
  92.2 6.4 %all_gather.18 = bf16[128,512]{1,0:T(8,128)(2,1)S(1)} all-gather(bf16[32,512]{1,0:T(8,128)(2,1)S(1)} %multiply_convert_fusion.1), channel_id=1, replica_groups=mesh['groups'=2,'ctx'=4,'head'=4] {'ctx'}, dimensions={0}, use_global_device_ids=true | all-gather | bytes 163840 | tf_op jit(solution)/shard_map/all_gather | solution.py:103
  98.9 20.0 %all-gather.8.cloned.1.call-done = bf16[4096,512]{1,0:T(8,128)(2,1)} async-done(((bf16[1024,512]{1,0:T(8,128)(2,1)}), bf16[4096,512]{1,0:T(8,128)(2,1)}) %all-gather.8.cloned.1.call-update) | async-done | bytes 4194320 | tf_op jit(solution)/shard_map/all_gather | solution.py:87
  118.9 10.1 %convert_reduce_fusion = (f32[32,512]{1,0:T(8,128)S(1)}, bf16[1024,512]{1,0:T(8,128)(2,1)}) fusion(bf16[1024,4096]{1,0:T(8,128)(2,1)} %add_convert_fusion, bf16[4096,512]{1,0:T(8,128)(2,1)} %all-gather.8.cloned.1.call-done), kind=kOutput, calls=%fused_computation.41 | convolution fusion | flops 4296523776 | bytes 13697024 | tf_op jit(solution)/shard_map/dot_general | solution.py:90
  129.0 5.4 %all_gather.19 = bf16[128,512]{1,0:T(8,128)(2,1)S(1)} all-gather(bf16[32,512]{1,0:T(8,128)(2,1)S(1)} %multiply_convert_fusion), channel_id=1, replica_groups=mesh['groups'=2,'ctx'=4,'head'=4] {'ctx'}, dimensions={0}, use_global_device_ids=true | all-gather | bytes 163840 | tf_op jit(solution)/shard_map/all_gather | solution.py:104
  134.9 5.2 %while.17 = (s32[]{:T(128)}, f32[4,1024]{1,0:T(4,128)S(1)}, f32[4,1024]{1,0:T(4,128)S(1)}, f32[4,1024,128]{2,1,0:T(8,128)S(1)}, s32[]{:T(128)}, /*index=5*/s32[]...) while((s32[]{:T(128)}, f32[4,1024]{1,0:T(4,128)S(1)}, ...), condition=%wide.region_6.7_spmd.clone, body=%wide.region_3.6_spmd.clone.sunk | while | flops 277116288 | bytes 12559769 | solution.py:64
  135.1 1.8 %fusion.61 = (f32[4,1024]{1,0:T(4,128)S(1)}, f32[4,1024,128]{1,2,0:T(8,128)S(1)}) fusion(pred[1024,128]{0,1:T(8,128)(4,1)S(1)} %compare_and_fusion.5, bf16[4,1024,128]{2,1,0:T(8,128)(2,1)} %get-tuple-element.322, bf16[4,128,128]{2,1,0:T(8,128)(2,1)S(1)} %get-tuple-element.323), kind=kOutput, calls=%fused_computation.4.clone.1 | convolution fusion | flops 135786496 | bytes 3424256 | tf_op jit(solution)/shard_map/while/body/hqd,hkd->hqk/dot_general | solution.py:18
  136.9 0.6 fusion.62
  137.5 2.5 %multiply_add_fusion.6 = f32[4,1024,128]{2,1,0:T(8,128)S(1)} fusion(f32[4,1024,128]{2,1,0:T(8,128)S(1)} %get-tuple-element.307, bf16[4,128,128]{2,1,0:T(8,128)(2,1)S(1)} %get-tuple-element.324, f32[4,1024,128]{1,2,0:T(8,128)S(1)} %get-tuple-element.286, f32[4,1024]{1,0:T(4,128)S(1)} %get-tuple-element.290, f32[4,1024]{1,0:T(4,128)S(1)} %get-tuple-element.291, ...), kind=kOutput, calls=%fused_computation.1.clone.1 | convolution fusion | flops 138412032 | bytes 6602752 | tf_op jit(solution)/shard_map/while/body/hqk,hkd->hqd/dot_general | solution.py:25
  140.0 1.9 %copy.32 = f32[4,1024,128]{1,2,0:T(8,128)} copy(f32[4,1024,128]{2,1,0:T(8,128)S(1)} %get-tuple-element.137) | data formatting | bytes 4194304 | tf_op jit(solution)/shard_map/while | solution.py:64
  141.9 1.5 copy.36
  143.4 5.0 %fusion.18 = (f32[4,1024]{1,0:T(4,128)S(1)}, f32[4,1024,1024]{1,2,0:T(8,128)S(1)}) fusion(pred[1024,1024]{0,1:T(8,128)(4,1)} %iota_compare_fusion, bf16[1024,4,128]{2,0,1:T(8,128)(2,1)} %bitcast.56, bf16[1024,512]{1,0:T(8,128)(2,1)} %get-tuple-element.213), kind=kOutput, calls=%fused_computation.35 | convolution fusion | flops 1086320640 | bytes 19939328 | tf_op jit(solution)/shard_map/hqd,hkd->hqk/dot_general | solution.py:18
  148.4 4.2 %fusion.19 = f32[4,1024]{1,0:T(4,128)S(1)} fusion(f32[4,1024,1024]{1,2,0:T(8,128)S(1)} %get-tuple-element.217, f32[4,1024]{1,0:T(4,128)S(1)} %get-tuple-element.216, pred[1024,1024]{0,1:T(8,128)(4,1)S(1)} %copy-done.1), kind=kLoop, calls=%fused_computation.36 | loop fusion | flops 20967424 | bytes 17858560 | tf_op jit(solution)/shard_map/reduce_sum | solution.py:24
  152.6 5.1 %divide_convert_fusion = bf16[4,1024,128]{1,2,0:T(8,128)(2,1)S(1)} fusion(f32[4,1024,128]{1,2,0:T(8,128)S(1)} %copy-done.2, bf16[4,1024,128]{1,2,0:T(8,128)(2,1)S(1)} %bitcast.57, f32[4,1024,1024]{1,2,0:T(8,128)S(1)} %get-tuple-element.217, f32[4,1024]{1,0:T(4,128)S(1)} %get-tuple-element.216, pred[1024,1024]{0,1:T(8,128)(4,1)S(1)} %copy-done.1, ...), kind=kOutput, calls=%fused_computation.43 | convolution fusion | flops 1097334784 | bytes 22085632 | tf_op jit(solution)/shard_map/hqk,hkd->hqd/dot_general | solution.py:25
  157.7 1.3 copy.33
  (26 shorter events, 1.0 us)
Async XLA Ops:
  6.5 3.5 %copy-start = (bf16[64,4096]{1,0:T(8,128)(2,1)S(1)}, bf16[64,4096]{1,0:T(8,128)(2,1)}, u32[]{:S(2)}) copy-start(bf16[64,4096]{1,0:T(8,128)(2,1)} %param.10) | copy-start | bytes 1572868
  6.5 3.5 %copy-start.3 = (s32[1024]{0:T(1024)S(1)}, s32[1024]{0:T(1024)}, u32[]{:S(2)}) copy-start(s32[1024]{0:T(1024)} %param.9) | copy-start | bytes 12292
  6.5 39.6 %all-gather.4.cloned.1.call-start = ((), (), s32[]{:S(2)}) async-start(), calls=%async_computation | async-start | bytes 5242880 | tf_op jit(solution)/shard_map/all_gather | solution.py:85
  7.3 74.9 %all-gather.6.cloned.1.call-start = ((), (), s32[]{:S(2)}) async-start(), calls=%async_computation.1 | async-start | bytes 5242880 | tf_op jit(solution)/shard_map/all_gather | solution.py:86
  8.0 110.9 %all-gather.8.cloned.1.call-start = ((), (), s32[]{:S(2)}) async-start(), calls=%async_computation.2 | async-start | bytes 5242880 | tf_op jit(solution)/shard_map/all_gather | solution.py:87
  143.4 5.0 %copy-start.1 = (pred[1024,1024]{0,1:T(8,128)(4,1)S(1)}, pred[1024,1024]{0,1:T(8,128)(4,1)}, u32[]{:S(2)}) copy-start(pred[1024,1024]{0,1:T(8,128)(4,1)} %iota_compare_fusion) | copy-start | bytes 3145732
  148.4 4.2 %copy-start.2 = (f32[4,1024,128]{1,2,0:T(8,128)S(1)}, f32[4,1024,128]{1,2,0:T(8,128)}, u32[]{:S(2)}) copy-start(f32[4,1024,128]{1,2,0:T(8,128)} %copy.32) | copy-start | bytes 6291460
Sparse Core Ops, SparseCore 0:
  8.9 37.1 all-gather.3
  47.7 34.4 all-gather.5
  83.7 35.1 all-gather.7
where the time goes:
time: 166 us
  waiting for transfers between devices  76.9 us (46%)
  matrix products  50.5 us (30%)
  between operations  13.3 us (8%)
  blocking collectives  11.8 us (7%)
  local copies, waits for them, and re-layouts  6.65 us (4%)
  other arithmetic  6.29 us (4%)
    dot_general x3, matrix products, on_device(): jnp.dot(hidden, piece, preferred_element_type=jnp.float32)  29.2 us
    all_gather x1, waiting for transfers between devices, on_device(): lax.all_gather(w_query, 'ctx', axis=0, tiled=True)  29.2 us
    all_gather x1, waiting for transfers between devices, on_device(): lax.all_gather(w_key, 'ctx', axis=0, tiled=True)  25.6 us
    all_gather x1, waiting for transfers between devices, on_device(): lax.all_gather(w_value, 'ctx', axis=0, tiled=True)  20 us
    dot_general x2, matrix products, partial_attend(): jnp.einsum('hqk,hkd->hqd', weights.astype(jnp.bfloat16), values, preferre...  7.61 us
    dot_general x1, matrix products, on_device(): jnp.dot(selector, tempo_table, preferred_element_type=jnp.float32)  6.89 us
    dot_general x2, matrix products, partial_attend(): jnp.einsum('hqd,hkd->hqk', queries, keys, preferred_element_type=jnp.floa...  6.75 us
    all_gather x1, blocking collectives, on_device(): lax.all_gather(own_keys, 'ctx', axis=0, tiled=True)  6.43 us
  transfers between devices with their start and end apart: 3, of which 3 were waited for; matrix products, arithmetic and copies ran while one was open for 17% of the time, Pallas kernels for 0%

commit v1 on v0

--- a/solution.py
+++ b/solution.py
@@ -8,6 +8,27 @@
 BEACONS = 32
 POOL = 32
 LOWEST = -1e30
+
+
+def collect(value, axis, dim):
+    peers, index, rows = (lax.axis_size(axis), lax.axis_index(axis), value.shape[dim])
+    right = [(i, (i + 1) % peers) for i in range(peers)]
+    behind = [(i, (i - 1) % peers) for i in range(peers)]
+    out = jnp.zeros((*value.shape[:dim], peers * rows, *value.shape[dim + 1 :]), value.dtype)
+    out = lax.dynamic_update_slice_in_dim(out, value, index * rows, axis=dim)
+    from_left = from_right = value
+    halfway = peers // 2
+    for step in range(1, halfway + 1):
+        from_left = lax.ppermute(from_left, axis, right)
+        out = lax.dynamic_update_slice_in_dim(
+            out, from_left, (index - step) % peers * rows, axis=dim
+        )
+        if step < peers - halfway:
+            from_right = lax.ppermute(from_right, axis, behind)
+            out = lax.dynamic_update_slice_in_dim(
+                out, from_right, (index + step) % peers * rows, axis=dim
+            )
+    return out
 
 
 def by_heads(matrix, heads_local):
@@ -83,7 +104,7 @@
     ).astype(jnp.bfloat16)
     pieces = (
         lax.all_gather(w_query, "ctx", axis=0, tiled=True),
-        lax.all_gather(w_key, "ctx", axis=0, tiled=True),
+        collect(w_key, "ctx", 0),
         lax.all_gather(w_value, "ctx", axis=0, tiled=True),
     )
     projected = tuple(

time: 166 us -> 147 us (0.89)
  waiting for transfers between devices: 76.9 us -> 53 us
  starting transfers between devices: 0.08 us -> 9.64 us
  matrix products: 50.5 us -> 42.5 us
  local copies, waits for them, and re-layouts: 6.65 us -> 9.53 us
    ppermute x0 -> x3, waiting for transfers between devices: none -> 41.5 us  [the longest x2 41.5 us: collect(): from_left = lax.ppermute(from_left, axis, right)]
    all_gather x1, waiting for transfers between devices: 29.2 us -> 0.02 us  [on_device(): lax.all_gather(w_query, 'ctx', axis=0, tiled=True)]
    all_gather x1 -> x0, waiting for transfers between devices: 25.6 us -> none  [on_device(): lax.all_gather(w_key, 'ctx', axis=0, tiled=True)]
    all_gather x1, waiting for transfers between devices: 20 us -> 10.1 us  [on_device(): lax.all_gather(w_value, 'ctx', axis=0, tiled=True)]
    ppermute x0 -> x3, starting transfers between devices: none -> 9.6 us  [the longest x2 7.62 us: collect(): from_left = lax.ppermute(from_left, axis, right)]
    dot_general x3, matrix products: 29.2 us -> 24.7 us  [on_device(): jnp.dot(hidden, piece, preferred_element_type=jnp.float32)]
    dynamic_update_slice x0 -> x4, local copies, waits for them, and re-layouts: none -> 2.45 us  [the longest x1 2.13 us: collect(): lax.dynamic_update_slice_in_dim(out, from_right, (index + step) % peers *...]
    dot_general x1, matrix products: 6.89 us -> 4.98 us  [on_device(): jnp.dot(selector, tempo_table, preferred_element_type=jnp.float32)]
  transfers between devices with their start and end apart: 3 -> 5, of which waited for: 3 -> 3; matrix products, arithmetic and copies ran while one was open for 17% -> 17% of each run, Pallas kernels for 0% -> 0%
where the time goes in v1:
time: 147 us
  waiting for transfers between devices  53 us (36%)
  matrix products  42.5 us (29%)
  between operations  13.6 us (9%)
  blocking collectives  12.3 us (8%)
  starting transfers between devices  9.64 us (7%)
  local copies, waits for them, and re-layouts  9.53 us (6%)
  other arithmetic  6.29 us (4%)
    ppermute x2, waiting for transfers between devices, collect(): from_left = lax.ppermute(from_left, axis, right)  41.5 us
    dot_general x3, matrix products, on_device(): jnp.dot(hidden, piece, preferred_element_type=jnp.float32)  24.7 us
    all_gather x1, waiting for transfers between devices, on_device(): lax.all_gather(w_value, 'ctx', axis=0, tiled=True)  10.1 us
    ppermute x2, starting transfers between devices, collect(): from_left = lax.ppermute(from_left, axis, right)  7.62 us
    dot_general x2, matrix products, partial_attend(): jnp.einsum('hqk,hkd->hqd', weights.astype(jnp.bfloat16), values, preferre...  7.61 us
    all_gather x1, blocking collectives, on_device(): lax.all_gather(own_keys, 'ctx', axis=0, tiled=True)  6.92 us
    all_gather x1, blocking collectives, on_device(): lax.all_gather(own_values, 'ctx', axis=0, tiled=True)  5.42 us
    dot_general x2, matrix products, partial_attend(): jnp.einsum('hqd,hkd->hqk', queries, keys, preferred_element_type=jnp.floa...  5.18 us
  transfers between devices with their start and end apart: 5, of which 3 were waited for; matrix products, arithmetic and copies ran while one was open for 17% of the time, Pallas kernels for 0%

profile of v1, /device:TPU:0, one launch (start us, length us, event | category | flops | bytes accessed | tf_op | source)
XLA Modules:
  0.0 147.2 jit_solution(5153105360735531426)
XLA Ops:
  6.5 0.7 all-gather.3.cloned.1.call-update
  7.3 0.7 all-gather.5.cloned.1.call-update
  8.6 2.0 %collective-permute-start.1 = (bf16[1024,512]{1,0:T(8,128)(2,1)}, bf16[1024,512]{1,0:T(8,128)(2,1)}, u32[]{:S(2)}, u32[]{:S(2)}) collective-permute-start(bf16[1024,512]{1,0:T(8,128)(2,1)} %param.12), channel_id=1, source_target_pairs={{0,12},{4,0},{8,4},{12,8},{1,13},{5,1},{9,5},{13,9},{2,14},{6,2},{... | collective-permute-start | bytes 3145736 | tf_op jit(solution)/shard_map/ppermute | solution.py:27
  10.5 1.3 iota_compare_fusion
  11.8 29.7 %collective-permute-done = bf16[1024,512]{1,0:T(8,128)(2,1)S(1)} collective-permute-done((bf16[1024,512]{1,0:T(8,128)(2,1)}, bf16[1024,512]{1,0:T(8,128)(2,1)S(1)}, u32[]{:S(2)}, u32[]{:S(2)}) %collective-permute-start) | collective-permute-done | bytes 1048608 | tf_op jit(solution)/shard_map/ppermute | solution.py:22
  41.5 7.1 %collective-permute-start.2 = (bf16[1024,512]{1,0:T(8,128)(2,1)S(1)}, bf16[1024,512]{1,0:T(8,128)(2,1)S(1)}, u32[]{:S(2)}, u32[]{:S(2)}) collective-permute-start(bf16[1024,512]{1,0:T(8,128)(2,1)S(1)} %collective-permute-done), channel_id=1, source_target_pairs={{0,4},{4,8},{8,12},{12,0},{1,5},{5,9},{9,13},{13,1},{2,6},{6,10},{... | collective-permute-start | bytes 3145736 | tf_op jit(solution)/shard_map/ppermute | solution.py:22
  49.0 5.0 %add_convert_fusion = bf16[1024,4096]{1,0:T(8,128)(2,1)S(1)} fusion(bf16[1024,4096]{1,0:T(8,128)(2,1)} %param.8, bf16[64,4096]{1,0:T(8,128)(2,1)S(1)} %copy-done, s32[1024]{0:T(1024)S(1)} %copy-done.7), kind=kOutput, calls=%fused_computation.34 | convolution fusion | flops 549519360 | bytes 17305600 | tf_op jit(solution)/shard_map/dot_general | solution.py:103
  54.1 2.1 %constant_dynamic-update-slice_fusion.1 = bf16[4096,512]{1,0:T(8,128)(2,1)S(1)} fusion(bf16[4096,512]{1,0:T(8,128)(2,1)S(1)} %constant_dynamic-update-slice_fusion.2, bf16[1024,512]{1,0:T(8,128)(2,1)} %collective-permute-done.1, s32[]{:T(128)S(6)} %select_n.82), kind=kLoop, calls=%fused_computation.60 | loop fusion | bytes 2097156 | tf_op jit(solution)/shard_map/dynamic_update_slice | solution.py:28
  56.3 11.8 %collective-permute-done.2 = bf16[1024,512]{1,0:T(8,128)(2,1)S(1)} collective-permute-done((bf16[1024,512]{1,0:T(8,128)(2,1)S(1)}, bf16[1024,512]{1,0:T(8,128)(2,1)S(1)}, u32[]{:S(2)}, u32[]{:S(2)}) %collective-permute-start.2) | collective-permute-done | bytes 1048608 | tf_op jit(solution)/shard_map/ppermute | solution.py:22
  68.2 5.5 %convert_reduce_fusion.1 = (f32[32,512]{1,0:T(8,128)S(1)}, bf16[1024,512]{1,0:T(8,128)(2,1)}) fusion(bf16[1024,4096]{1,0:T(8,128)(2,1)S(1)} %add_convert_fusion, bf16[4096,512]{1,0:T(8,128)(2,1)S(1)} %constant_dynamic-update-slice_fusion), kind=kOutput, calls=%fused_computation.42 | convolution fusion | flops 4296523776 | bytes 13697024 | tf_op jit(solution)/shard_map/dot_general | solution.py:111
  73.7 6.9 %all_gather.14 = bf16[128,512]{1,0:T(8,128)(2,1)S(1)} all-gather(bf16[32,512]{1,0:T(8,128)(2,1)S(1)} %multiply_convert_fusion.1), channel_id=1, replica_groups=mesh['groups'=2,'ctx'=4,'head'=4] {'ctx'}, dimensions={0}, use_global_device_ids=true | all-gather | bytes 163840 | tf_op jit(solution)/shard_map/all_gather | solution.py:124
  80.9 9.1 %convolution_convert_fusion.2 = bf16[1024,512]{0,1:T(8,128)(2,1)S(1)} fusion(bf16[1024,4096]{1,0:T(8,128)(2,1)} %copy-done.2, bf16[4096,512]{1,0:T(8,128)(2,1)} %all-gather.3.cloned.1.call-done), kind=kOutput, calls=%fused_computation.46 | convolution fusion | flops 4295491584 | bytes 13631488 | tf_op jit(solution)/shard_map/dot_general | solution.py:111
  90.1 0.7 copy.24
  90.7 10.1 %all-gather.5.cloned.1.call-done = bf16[4096,512]{1,0:T(8,128)(2,1)} async-done(((bf16[1024,512]{1,0:T(8,128)(2,1)}), bf16[4096,512]{1,0:T(8,128)(2,1)}) %all-gather.5.cloned.1.call-update) | async-done | bytes 4194320 | tf_op jit(solution)/shard_map/all_gather | solution.py:108
  100.8 10.1 %convert_reduce_fusion = (f32[32,512]{1,0:T(8,128)S(1)}, bf16[1024,512]{1,0:T(8,128)(2,1)}) fusion(bf16[1024,4096]{1,0:T(8,128)(2,1)} %copy-done.2, bf16[4096,512]{1,0:T(8,128)(2,1)} %all-gather.5.cloned.1.call-done), kind=kOutput, calls=%fused_computation.41 | convolution fusion | flops 4296523776 | bytes 13697024 | tf_op jit(solution)/shard_map/dot_general | solution.py:111
  110.9 5.4 %all_gather.15 = bf16[128,512]{1,0:T(8,128)(2,1)S(1)} all-gather(bf16[32,512]{1,0:T(8,128)(2,1)S(1)} %multiply_convert_fusion), channel_id=1, replica_groups=mesh['groups'=2,'ctx'=4,'head'=4] {'ctx'}, dimensions={0}, use_global_device_ids=true | all-gather | bytes 163840 | tf_op jit(solution)/shard_map/all_gather | solution.py:125
  116.8 4.1 %while.17 = (s32[]{:T(128)}, f32[4,1024]{1,0:T(4,128)S(1)}, f32[4,1024]{1,0:T(4,128)S(1)}, f32[4,1024,128]{2,1,0:T(8,128)S(1)}, s32[]{:T(128)}, /*index=5*/s32[]...) while((s32[]{:T(128)}, f32[4,1024]{1,0:T(4,128)S(1)}, ...), condition=%wide.region_6.7_spmd.clone, body=%wide.region_3.6_spmd.clone.sunk | while | flops 277116288 | bytes 12559769 | solution.py:85
  118.1 2.5 %multiply_add_fusion.6 = f32[4,1024,128]{2,1,0:T(8,128)S(1)} fusion(f32[4,1024,128]{2,1,0:T(8,128)S(1)} %get-tuple-element.307, bf16[4,128,128]{2,1,0:T(8,128)(2,1)S(1)} %get-tuple-element.324, f32[4,1024,128]{1,2,0:T(8,128)S(1)} %get-tuple-element.286, f32[4,1024]{1,0:T(4,128)S(1)} %get-tuple-element.290, f32[4,1024]{1,0:T(4,128)S(1)} %get-tuple-element.291, ...), kind=kOutput, calls=%fused_computation.1.clone.1 | convolution fusion | flops 138412032 | bytes 6602752 | tf_op jit(solution)/shard_map/while/body/hqk,hkd->hqd/dot_general | solution.py:46
  120.9 1.9 %copy.32 = f32[4,1024,128]{1,2,0:T(8,128)} copy(f32[4,1024,128]{2,1,0:T(8,128)S(1)} %get-tuple-element.137) | data formatting | bytes 4194304 | tf_op jit(solution)/shard_map/while | solution.py:85
  122.8 2.2 %copy.36 = bf16[1024,512]{0,1:T(8,128)(2,1)} copy(bf16[1024,512]{1,0:T(8,128)(2,1)} %get-tuple-element.215) | data formatting | bytes 2097152 | tf_op jit(solution)/shard_map/reshape | solution.py:35
  125.0 4.6 %fusion.18 = (f32[4,1024]{1,0:T(4,128)S(1)}, f32[4,1024,1024]{1,2,0:T(8,128)S(1)}) fusion(pred[1024,1024]{0,1:T(8,128)(4,1)} %iota_compare_fusion, bf16[1024,4,128]{2,0,1:T(8,128)(2,1)S(1)} %bitcast.56, bf16[1024,512]{1,0:T(8,128)(2,1)} %get-tuple-element.213), kind=kOutput, calls=%fused_computation.35 | convolution fusion | flops 1086320640 | bytes 19939328 | tf_op jit(solution)/shard_map/hqd,hkd->hqk/dot_general | solution.py:39
  129.7 4.2 %fusion.19 = f32[4,1024]{1,0:T(4,128)S(1)} fusion(f32[4,1024,1024]{1,2,0:T(8,128)S(1)} %get-tuple-element.217, f32[4,1024]{1,0:T(4,128)S(1)} %get-tuple-element.216, pred[1024,1024]{0,1:T(8,128)(4,1)S(1)} %copy-done.3), kind=kLoop, calls=%fused_computation.36 | loop fusion | flops 20967424 | bytes 17858560 | tf_op jit(solution)/shard_map/reduce_sum | solution.py:45
  134.0 5.1 %divide_convert_fusion = bf16[4,1024,128]{1,2,0:T(8,128)(2,1)S(1)} fusion(f32[4,1024,128]{1,2,0:T(8,128)S(1)} %copy-done.4, bf16[4,1024,128]{1,2,0:T(8,128)(2,1)S(1)} %bitcast.57, f32[4,1024,1024]{1,2,0:T(8,128)S(1)} %get-tuple-element.217, f32[4,1024]{1,0:T(4,128)S(1)} %get-tuple-element.216, pred[1024,1024]{0,1:T(8,128)(4,1)S(1)} %copy-done.3, ...), kind=kOutput, calls=%fused_computation.43 | convolution fusion | flops 1097334784 | bytes 22085632 | tf_op jit(solution)/shard_map/hqk,hkd->hqd/dot_general | solution.py:46
  139.0 1.3 copy.33
  (42 shorter events, 3.2 us)
Async XLA Ops:
  6.5 42.5 %copy-start = (bf16[64,4096]{1,0:T(8,128)(2,1)S(1)}, bf16[64,4096]{1,0:T(8,128)(2,1)}, u32[]{:S(2)}) copy-start(bf16[64,4096]{1,0:T(8,128)(2,1)} %param.10) | copy-start | bytes 1572868
  6.5 42.4 %copy-start.5 = (bf16[1024,512]{1,0:T(8,128)(2,1)S(1)}, bf16[1024,512]{1,0:T(8,128)(2,1)}, u32[]{:S(2)}) copy-start(bf16[1024,512]{1,0:T(8,128)(2,1)} %param.12) | copy-start | bytes 3145732
  6.5 74.4 %all-gather.3.cloned.1.call-start = ((), (), s32[]{:S(2)}) async-start(), calls=%async_computation | async-start | bytes 5242880 | tf_op jit(solution)/shard_map/all_gather | solution.py:106
  7.3 41.8 %copy-start.7 = (s32[1024]{0:T(1024)S(1)}, s32[1024]{0:T(1024)}, u32[]{:S(2)}) copy-start(s32[1024]{0:T(1024)} %param.9) | copy-start | bytes 12292
  7.3 93.5 %all-gather.5.cloned.1.call-start = ((), (), s32[]{:S(2)}) async-start(), calls=%async_computation.1 | async-start | bytes 5242880 | tf_op jit(solution)/shard_map/all_gather | solution.py:108
  8.0 33.5 %collective-permute-start = (bf16[1024,512]{1,0:T(8,128)(2,1)}, bf16[1024,512]{1,0:T(8,128)(2,1)S(1)}, u32[]{:S(2)}, u32[]{:S(2)}) collective-permute-start(bf16[1024,512]{1,0:T(8,128)(2,1)} %param.12), channel_id=1, source_target_pairs={{0,4},{4,8},{8,12},{12,0},{1,5},{5,9},{9,13},{13,1},{2,6},{6,10},{... | collective-permute-start | bytes 3145736 | tf_op jit(solution)/shard_map/ppermute | solution.py:22
  8.6 45.6 %collective-permute-start.1 = (bf16[1024,512]{1,0:T(8,128)(2,1)}, bf16[1024,512]{1,0:T(8,128)(2,1)}, u32[]{:S(2)}, u32[]{:S(2)}) collective-permute-start(bf16[1024,512]{1,0:T(8,128)(2,1)} %param.12), channel_id=1, source_target_pairs={{0,12},{4,0},{8,4},{12,8},{1,13},{5,1},{9,5},{13,9},{2,14},{6,2},{... | collective-permute-start | bytes 3145736 | tf_op jit(solution)/shard_map/ppermute | solution.py:27
  41.5 26.6 %collective-permute-start.2 = (bf16[1024,512]{1,0:T(8,128)(2,1)S(1)}, bf16[1024,512]{1,0:T(8,128)(2,1)S(1)}, u32[]{:S(2)}, u32[]{:S(2)}) collective-permute-start(bf16[1024,512]{1,0:T(8,128)(2,1)S(1)} %collective-permute-done), channel_id=1, source_target_pairs={{0,4},{4,8},{8,12},{12,0},{1,5},{5,9},{9,13},{13,1},{2,6},{6,10},{... | collective-permute-start | bytes 3145736 | tf_op jit(solution)/shard_map/ppermute | solution.py:22
  54.0 19.7 %copy-start.2 = (bf16[1024,4096]{1,0:T(8,128)(2,1)}, bf16[1024,4096]{1,0:T(8,128)(2,1)S(1)}, u32[]{:S(2)}) copy-start(bf16[1024,4096]{1,0:T(8,128)(2,1)S(1)} %add_convert_fusion) | copy-start | bytes 25165828
  125.0 4.6 %copy-start.3 = (pred[1024,1024]{0,1:T(8,128)(4,1)S(1)}, pred[1024,1024]{0,1:T(8,128)(4,1)}, u32[]{:S(2)}) copy-start(pred[1024,1024]{0,1:T(8,128)(4,1)} %iota_compare_fusion) | copy-start | bytes 3145732
  129.7 4.2 %copy-start.4 = (f32[4,1024,128]{1,2,0:T(8,128)S(1)}, f32[4,1024,128]{1,2,0:T(8,128)}, u32[]{:S(2)}) copy-start(f32[4,1024,128]{1,2,0:T(8,128)} %copy.32) | copy-start | bytes 6291460
  129.7 4.2 %copy-start.6 = (bf16[1024,512]{0,1:T(8,128)(2,1)S(1)}, bf16[1024,512]{0,1:T(8,128)(2,1)}, u32[]{:S(2)}) copy-start(bf16[1024,512]{0,1:T(8,128)(2,1)} %copy.36) | copy-start | bytes 3145732
  134.0 6.4 %copy-start.1 = (bf16[64,4096]{1,0:T(8,128)(2,1)S(1)}, bf16[64,4096]{1,0:T(8,128)(2,1)}, u32[]{:S(2)}) copy-start(bf16[64,4096]{1,0:T(8,128)(2,1)} %param.10) | copy-start | bytes 1572868
Sparse Core Ops, SparseCore 0:
  8.9 54.9 all-gather.2
  65.4 35.3 all-gather.4
